TPU v7x, 32 devices: a whole 2x2x4 slice. The times are simulated.
32 devices in a mesh: band: 2 (over x), blk: 16 (over z, y, core).
Axes of the slice: x: 2, y: 2, z: 4, core: 2. Of those that a mesh axis runs over, the one named last changes fastest.
Arguments:
- spectra: bfloat16 [768, 4, 1024], P(('band', 'blk')), parts along dimension 0, may hold values from -6 to 6
- counts: int32 [768, 4], P(('band', 'blk')), parts along dimension 0, may hold values from 0 to 12
Outputs:
- correlograms: bfloat16 [768, 16, 1024], P(('band', 'blk')), parts along dimension 0
There are 2 independent parts, one for each index of `band`. A program takes and returns all parts, laid end to end along the dimension named above; each array names one. Nothing has to cross between parts.
All inputs are finite; a program needn't handle non-finite values.
Results may differ from a plain program's by a relative error of at most 0.0085.
Values may be sent and summed in bfloat16 or wider, within the bound.
A program may use at most 64 MiB of HBM per device.

v0:
```python
import math

import jax
import jax.numpy as jnp
from jax import lax
from jax.sharding import PartitionSpec as P

LAG = 1024


def from_behind(value, axis, steps):
    count = lax.axis_size(axis)
    pairs = [(source, (source + steps) % count) for source in range(count)]
    return lax.ppermute(value, axis, pairs)


def lag_table():
    bins = jnp.arange(LAG // 2, dtype=jnp.int32)
    taps = jnp.arange(LAG, dtype=jnp.int32) - LAG // 2
    phase = bins[:, None] * taps[None, :] % LAG
    angle = phase.astype(jnp.float32) * (2.0 * math.pi / LAG)
    return jnp.concatenate([jnp.cos(angle), jnp.sin(angle)], 0).astype(jnp.bfloat16)


def split_parts(block, block_counts):
    half = block.shape[2] // 2
    real_part = block[:, :, :half].astype(jnp.float32)
    imag_part = block[:, :, half:].astype(jnp.float32)
    inverse = lax.rsqrt(real_part * real_part + imag_part * imag_part + 0.25)
    return (
        real_part,
        imag_part,
        real_part * inverse,
        imag_part * inverse,
        block_counts.astype(jnp.float32),
    )


def pair_beams(own, own_counts, other, other_counts):
    ra, ia, pa, qa, ca = split_parts(own, own_counts)
    rb, ib, pb, qb, cb = split_parts(other, other_counts)
    acc_re = 0.0
    acc_im = 0.0
    coh_re = 0.0
    coh_im = 0.0
    weight_sum = 0.0
    for seg in range(ra.shape[1]):
        weight = jnp.minimum(ca[:, None, seg], cb[None, :, seg])[:, :, None]
        xa_re = ra[:, None, seg, :]
        xa_im = ia[:, None, seg, :]
        xb_re = rb[None, :, seg, :]
        xb_im = ib[None, :, seg, :]
        acc_re = acc_re + weight * (xa_re * xb_re + xa_im * xb_im)
        acc_im = acc_im + weight * (xa_im * xb_re - xa_re * xb_im)
        ya_re = pa[:, None, seg, :]
        ya_im = qa[:, None, seg, :]
        yb_re = pb[None, :, seg, :]
        yb_im = qb[None, :, seg, :]
        coh_re = coh_re + weight * (ya_re * yb_re + ya_im * yb_im)
        coh_im = coh_im + weight * (ya_im * yb_re - ya_re * yb_im)
        weight_sum = weight_sum + weight
    total = jnp.maximum(weight_sum, 1.0)
    factor = (coh_re * coh_re + coh_im * coh_im) / (total * total * total)
    stack_re = acc_re * factor
    stack_im = acc_im * factor
    forward = jnp.concatenate([jnp.sum(stack_re, 1), jnp.sum(stack_im, 1)], -1)
    backward = jnp.concatenate([jnp.sum(stack_re, 0), -jnp.sum(stack_im, 0)], -1)
    return (forward, backward)


def lag_traces(beam, table):
    rows = jnp.dot(beam.reshape(-1, beam.shape[2]), table, preferred_element_type=jnp.float32)
    return rows.astype(jnp.bfloat16).reshape(beam.shape[0], beam.shape[1], table.shape[1])


def shards(spectra, counts):
    stations = spectra.shape[0]
    spread = spectra.shape[2]
    blocks_n = lax.axis_size("blk")
    table = lag_table()
    own_counts = counts.astype(jnp.bfloat16)
    first, unused = pair_beams(spectra, own_counts, spectra, own_counts)
    forward = jnp.zeros((stations, blocks_n, spread), jnp.bfloat16)
    forward = lax.dynamic_update_slice_in_dim(forward, first.astype(jnp.bfloat16)[:, None], 0, 1)

    def turn_full(offset, carry):
        visitor, visitor_counts, ahead = carry
        visitor, visitor_counts = from_behind((visitor, visitor_counts), "blk", -1)
        towards, unused_back = pair_beams(spectra, own_counts, visitor, visitor_counts)
        ahead = lax.dynamic_update_slice_in_dim(
            ahead, towards.astype(jnp.bfloat16)[:, None], offset, 1
        )
        return (visitor, visitor_counts, ahead)

    state = lax.fori_loop(1, blocks_n, turn_full, (spectra, own_counts, forward))
    traces = lag_traces(state[2], table)
    values = traces.astype(jnp.float32)
    scale = jnp.sqrt(jnp.mean(values * values, -1, keepdims=True) + 1e-06)
    return (values / scale).astype(jnp.bfloat16)


def solution(mesh):
    return jax.shard_map(
        shards,
        mesh=mesh,
        in_specs=(P(("band", "blk"), None, None), P(("band", "blk"), None)),
        out_specs=P(("band", "blk"), None, None),
        check_vma=False,
    )
```

profile of v0, /device:TPU:1, one launch (start us, length us, event | category | flops | bytes accessed | tf_op | source)
XLA Modules:
  0.0 236.5 jit_solution(13762940813540193526)
XLA Ops:
  2.0 3.3 %multiply_reduce_fusion.4 = bf16[24,512]{1,0:T(8,128)(2,1)S(1)} fusion(f32[24,512]{1,0:T(8,128)S(1)} %get-tuple-element.264, f32[24,512]{1,0:T(8,128)S(1)} %get-tuple-element.284, f32[24,24]{1,0:T(8,128)S(1)} %get-tuple-element.276, f32[24,512]{1,0:T(8,128)S(1)} %get-tuple-element.265, f32[24,512]{1,0:T(8,128)S(1)} %get-tuple-element.283, ...), kind=kLoop, calls=%fused_computation.84 | loop fusion | flops 18567168 | bytes 822528 | tf_op jit(solution)/shard_map/reduce_sum | solution.py:66
  5.3 3.3 %multiply_reduce_fusion.3 = bf16[24,512]{1,0:T(8,128)(2,1)S(1)} fusion(f32[24,512]{1,0:T(8,128)S(1)} %get-tuple-element.264, f32[24,512]{1,0:T(8,128)S(1)} %get-tuple-element.284, f32[24,24]{1,0:T(8,128)S(1)} %get-tuple-element.276, f32[24,512]{1,0:T(8,128)S(1)} %get-tuple-element.265, f32[24,512]{1,0:T(8,128)S(1)} %get-tuple-element.283, ...), kind=kLoop, calls=%fused_computation.83 | loop fusion | flops 18567168 | bytes 822528 | tf_op jit(solution)/shard_map/reduce_sum | solution.py:66
  8.6 216.6 %while.19 = (s32[]{:T(128)}, bf16[24,4,1024]{2,0,1:T(8,128)(2,1)S(1)}, bf16[24,4]{0,1:T(4,128)(2,1)S(1)}, bf16[24,16,1024]{2,0,1:T(8,128)(2,1)S(1)}, bf16[24,4]{...) while((s32[]{:T(128)}, ...), condition=%wide.region_5.6_spmd, body=%wide.region_2.5_spmd.sunk | while | flops 38221636 | bytes 10017235 | solution.py:95
  8.7 5.4 %collective-permute-start = (bf16[24,4,1024]{2,0,1:T(8,128)(2,1)S(1)}, bf16[24,4,1024]{2,0,1:T(8,128)(2,1)S(1)}, u32[]{:S(2)}, u32[]{:S(2)}) collective-permute-start(bf16[24,4,1024]{2,0,1:T(8,128)(2,1)S(1)} %get-tuple-element.443), channel_id=1, source_target_pairs={{0,15},{1,0},{2,1},{3,2},{4,3},{5,4},{6,5},{7,6},{8,7},{9,8},{10,9... | collective-permute-start | bytes 589832 | tf_op jit(solution)/shard_map/while/body/eval_jaxpr/ppermute | solution.py:14
  24.7 4.6 %collective-permute-start = (bf16[24,4,1024]{2,0,1:T(8,128)(2,1)S(1)}, bf16[24,4,1024]{2,0,1:T(8,128)(2,1)S(1)}, u32[]{:S(2)}, u32[]{:S(2)}) collective-permute-start(bf16[24,4,1024]{2,0,1:T(8,128)(2,1)S(1)} %get-tuple-element.443), channel_id=1, source_target_pairs={{0,15},{1,0},{2,1},{3,2},{4,3},{5,4},{6,5},{7,6},{8,7},{9,8},{10,9... | collective-permute-start | bytes 589832 | tf_op jit(solution)/shard_map/while/body/eval_jaxpr/ppermute | solution.py:14
  39.2 4.6 %collective-permute-start = (bf16[24,4,1024]{2,0,1:T(8,128)(2,1)S(1)}, bf16[24,4,1024]{2,0,1:T(8,128)(2,1)S(1)}, u32[]{:S(2)}, u32[]{:S(2)}) collective-permute-start(bf16[24,4,1024]{2,0,1:T(8,128)(2,1)S(1)} %get-tuple-element.443), channel_id=1, source_target_pairs={{0,15},{1,0},{2,1},{3,2},{4,3},{5,4},{6,5},{7,6},{8,7},{9,8},{10,9... | collective-permute-start | bytes 589832 | tf_op jit(solution)/shard_map/while/body/eval_jaxpr/ppermute | solution.py:14
  53.7 4.6 %collective-permute-start = (bf16[24,4,1024]{2,0,1:T(8,128)(2,1)S(1)}, bf16[24,4,1024]{2,0,1:T(8,128)(2,1)S(1)}, u32[]{:S(2)}, u32[]{:S(2)}) collective-permute-start(bf16[24,4,1024]{2,0,1:T(8,128)(2,1)S(1)} %get-tuple-element.443), channel_id=1, source_target_pairs={{0,15},{1,0},{2,1},{3,2},{4,3},{5,4},{6,5},{7,6},{8,7},{9,8},{10,9... | collective-permute-start | bytes 589832 | tf_op jit(solution)/shard_map/while/body/eval_jaxpr/ppermute | solution.py:14
  62.7 3.2 %multiply_reduce_fusion.7 = bf16[24,512]{1,0:T(8,128)(2,1)S(1)} fusion(f32[24,512]{1,0:T(8,128)S(1)} %get-tuple-element.382, f32[24,512]{1,0:T(8,128)S(1)} %get-tuple-element.385, f32[24,512]{1,0:T(8,128)S(1)} %get-tuple-element.386, f32[24,512]{1,0:T(8,128)S(1)} %get-tuple-element.387, f32[24,24]{1,0:T(8,128)S(1)} %get-tuple-element.396, ...), kind=kLoop, calls=%fused_computation.clone.1 | loop fusion | flops 18567168 | bytes 1608960 | tf_op jit(solution)/shard_map/while/body/eval_jaxpr/reduce_sum | solution.py:66
  68.1 4.6 %collective-permute-start = (bf16[24,4,1024]{2,0,1:T(8,128)(2,1)S(1)}, bf16[24,4,1024]{2,0,1:T(8,128)(2,1)S(1)}, u32[]{:S(2)}, u32[]{:S(2)}) collective-permute-start(bf16[24,4,1024]{2,0,1:T(8,128)(2,1)S(1)} %get-tuple-element.443), channel_id=1, source_target_pairs={{0,15},{1,0},{2,1},{3,2},{4,3},{5,4},{6,5},{7,6},{8,7},{9,8},{10,9... | collective-permute-start | bytes 589832 | tf_op jit(solution)/shard_map/while/body/eval_jaxpr/ppermute | solution.py:14
  77.2 3.2 %multiply_reduce_fusion.7 = bf16[24,512]{1,0:T(8,128)(2,1)S(1)} fusion(f32[24,512]{1,0:T(8,128)S(1)} %get-tuple-element.382, f32[24,512]{1,0:T(8,128)S(1)} %get-tuple-element.385, f32[24,512]{1,0:T(8,128)S(1)} %get-tuple-element.386, f32[24,512]{1,0:T(8,128)S(1)} %get-tuple-element.387, f32[24,24]{1,0:T(8,128)S(1)} %get-tuple-element.396, ...), kind=kLoop, calls=%fused_computation.clone.1 | loop fusion | flops 18567168 | bytes 1608960 | tf_op jit(solution)/shard_map/while/body/eval_jaxpr/reduce_sum | solution.py:66
  82.6 4.6 %collective-permute-start = (bf16[24,4,1024]{2,0,1:T(8,128)(2,1)S(1)}, bf16[24,4,1024]{2,0,1:T(8,128)(2,1)S(1)}, u32[]{:S(2)}, u32[]{:S(2)}) collective-permute-start(bf16[24,4,1024]{2,0,1:T(8,128)(2,1)S(1)} %get-tuple-element.443), channel_id=1, source_target_pairs={{0,15},{1,0},{2,1},{3,2},{4,3},{5,4},{6,5},{7,6},{8,7},{9,8},{10,9... | collective-permute-start | bytes 589832 | tf_op jit(solution)/shard_map/while/body/eval_jaxpr/ppermute | solution.py:14
  91.7 3.2 %multiply_reduce_fusion.7 = bf16[24,512]{1,0:T(8,128)(2,1)S(1)} fusion(f32[24,512]{1,0:T(8,128)S(1)} %get-tuple-element.382, f32[24,512]{1,0:T(8,128)S(1)} %get-tuple-element.385, f32[24,512]{1,0:T(8,128)S(1)} %get-tuple-element.386, f32[24,512]{1,0:T(8,128)S(1)} %get-tuple-element.387, f32[24,24]{1,0:T(8,128)S(1)} %get-tuple-element.396, ...), kind=kLoop, calls=%fused_computation.clone.1 | loop fusion | flops 18567168 | bytes 1608960 | tf_op jit(solution)/shard_map/while/body/eval_jaxpr/reduce_sum | solution.py:66
  97.1 4.6 %collective-permute-start = (bf16[24,4,1024]{2,0,1:T(8,128)(2,1)S(1)}, bf16[24,4,1024]{2,0,1:T(8,128)(2,1)S(1)}, u32[]{:S(2)}, u32[]{:S(2)}) collective-permute-start(bf16[24,4,1024]{2,0,1:T(8,128)(2,1)S(1)} %get-tuple-element.443), channel_id=1, source_target_pairs={{0,15},{1,0},{2,1},{3,2},{4,3},{5,4},{6,5},{7,6},{8,7},{9,8},{10,9... | collective-permute-start | bytes 589832 | tf_op jit(solution)/shard_map/while/body/eval_jaxpr/ppermute | solution.py:14
  106.1 3.2 %multiply_reduce_fusion.7 = bf16[24,512]{1,0:T(8,128)(2,1)S(1)} fusion(f32[24,512]{1,0:T(8,128)S(1)} %get-tuple-element.382, f32[24,512]{1,0:T(8,128)S(1)} %get-tuple-element.385, f32[24,512]{1,0:T(8,128)S(1)} %get-tuple-element.386, f32[24,512]{1,0:T(8,128)S(1)} %get-tuple-element.387, f32[24,24]{1,0:T(8,128)S(1)} %get-tuple-element.396, ...), kind=kLoop, calls=%fused_computation.clone.1 | loop fusion | flops 18567168 | bytes 1608960 | tf_op jit(solution)/shard_map/while/body/eval_jaxpr/reduce_sum | solution.py:66
  111.6 4.6 %collective-permute-start = (bf16[24,4,1024]{2,0,1:T(8,128)(2,1)S(1)}, bf16[24,4,1024]{2,0,1:T(8,128)(2,1)S(1)}, u32[]{:S(2)}, u32[]{:S(2)}) collective-permute-start(bf16[24,4,1024]{2,0,1:T(8,128)(2,1)S(1)} %get-tuple-element.443), channel_id=1, source_target_pairs={{0,15},{1,0},{2,1},{3,2},{4,3},{5,4},{6,5},{7,6},{8,7},{9,8},{10,9... | collective-permute-start | bytes 589832 | tf_op jit(solution)/shard_map/while/body/eval_jaxpr/ppermute | solution.py:14
  126.1 4.6 %collective-permute-start = (bf16[24,4,1024]{2,0,1:T(8,128)(2,1)S(1)}, bf16[24,4,1024]{2,0,1:T(8,128)(2,1)S(1)}, u32[]{:S(2)}, u32[]{:S(2)}) collective-permute-start(bf16[24,4,1024]{2,0,1:T(8,128)(2,1)S(1)} %get-tuple-element.443), channel_id=1, source_target_pairs={{0,15},{1,0},{2,1},{3,2},{4,3},{5,4},{6,5},{7,6},{8,7},{9,8},{10,9... | collective-permute-start | bytes 589832 | tf_op jit(solution)/shard_map/while/body/eval_jaxpr/ppermute | solution.py:14
  140.6 4.6 %collective-permute-start = (bf16[24,4,1024]{2,0,1:T(8,128)(2,1)S(1)}, bf16[24,4,1024]{2,0,1:T(8,128)(2,1)S(1)}, u32[]{:S(2)}, u32[]{:S(2)}) collective-permute-start(bf16[24,4,1024]{2,0,1:T(8,128)(2,1)S(1)} %get-tuple-element.443), channel_id=1, source_target_pairs={{0,15},{1,0},{2,1},{3,2},{4,3},{5,4},{6,5},{7,6},{8,7},{9,8},{10,9... | collective-permute-start | bytes 589832 | tf_op jit(solution)/shard_map/while/body/eval_jaxpr/ppermute | solution.py:14
  149.6 3.2 %multiply_reduce_fusion.7 = bf16[24,512]{1,0:T(8,128)(2,1)S(1)} fusion(f32[24,512]{1,0:T(8,128)S(1)} %get-tuple-element.382, f32[24,512]{1,0:T(8,128)S(1)} %get-tuple-element.385, f32[24,512]{1,0:T(8,128)S(1)} %get-tuple-element.386, f32[24,512]{1,0:T(8,128)S(1)} %get-tuple-element.387, f32[24,24]{1,0:T(8,128)S(1)} %get-tuple-element.396, ...), kind=kLoop, calls=%fused_computation.clone.1 | loop fusion | flops 18567168 | bytes 1608960 | tf_op jit(solution)/shard_map/while/body/eval_jaxpr/reduce_sum | solution.py:66
  155.1 4.6 %collective-permute-start = (bf16[24,4,1024]{2,0,1:T(8,128)(2,1)S(1)}, bf16[24,4,1024]{2,0,1:T(8,128)(2,1)S(1)}, u32[]{:S(2)}, u32[]{:S(2)}) collective-permute-start(bf16[24,4,1024]{2,0,1:T(8,128)(2,1)S(1)} %get-tuple-element.443), channel_id=1, source_target_pairs={{0,15},{1,0},{2,1},{3,2},{4,3},{5,4},{6,5},{7,6},{8,7},{9,8},{10,9... | collective-permute-start | bytes 589832 | tf_op jit(solution)/shard_map/while/body/eval_jaxpr/ppermute | solution.py:14
  169.5 4.6 %collective-permute-start = (bf16[24,4,1024]{2,0,1:T(8,128)(2,1)S(1)}, bf16[24,4,1024]{2,0,1:T(8,128)(2,1)S(1)}, u32[]{:S(2)}, u32[]{:S(2)}) collective-permute-start(bf16[24,4,1024]{2,0,1:T(8,128)(2,1)S(1)} %get-tuple-element.443), channel_id=1, source_target_pairs={{0,15},{1,0},{2,1},{3,2},{4,3},{5,4},{6,5},{7,6},{8,7},{9,8},{10,9... | collective-permute-start | bytes 589832 | tf_op jit(solution)/shard_map/while/body/eval_jaxpr/ppermute | solution.py:14
  184.0 4.6 %collective-permute-start = (bf16[24,4,1024]{2,0,1:T(8,128)(2,1)S(1)}, bf16[24,4,1024]{2,0,1:T(8,128)(2,1)S(1)}, u32[]{:S(2)}, u32[]{:S(2)}) collective-permute-start(bf16[24,4,1024]{2,0,1:T(8,128)(2,1)S(1)} %get-tuple-element.443), channel_id=1, source_target_pairs={{0,15},{1,0},{2,1},{3,2},{4,3},{5,4},{6,5},{7,6},{8,7},{9,8},{10,9... | collective-permute-start | bytes 589832 | tf_op jit(solution)/shard_map/while/body/eval_jaxpr/ppermute | solution.py:14
  198.5 4.6 %collective-permute-start = (bf16[24,4,1024]{2,0,1:T(8,128)(2,1)S(1)}, bf16[24,4,1024]{2,0,1:T(8,128)(2,1)S(1)}, u32[]{:S(2)}, u32[]{:S(2)}) collective-permute-start(bf16[24,4,1024]{2,0,1:T(8,128)(2,1)S(1)} %get-tuple-element.443), channel_id=1, source_target_pairs={{0,15},{1,0},{2,1},{3,2},{4,3},{5,4},{6,5},{7,6},{8,7},{9,8},{10,9... | collective-permute-start | bytes 589832 | tf_op jit(solution)/shard_map/while/body/eval_jaxpr/ppermute | solution.py:14
  213.0 4.6 %collective-permute-start = (bf16[24,4,1024]{2,0,1:T(8,128)(2,1)S(1)}, bf16[24,4,1024]{2,0,1:T(8,128)(2,1)S(1)}, u32[]{:S(2)}, u32[]{:S(2)}) collective-permute-start(bf16[24,4,1024]{2,0,1:T(8,128)(2,1)S(1)} %get-tuple-element.443), channel_id=1, source_target_pairs={{0,15},{1,0},{2,1},{3,2},{4,3},{5,4},{6,5},{7,6},{8,7},{9,8},{10,9... | collective-permute-start | bytes 589832 | tf_op jit(solution)/shard_map/while/body/eval_jaxpr/ppermute | solution.py:14
  225.7 8.5 %cosine_convert_fusion = (bf16[512,1024]{1,0:T(8,128)(2,1)S(1)}, bf16[512,1024]{1,0:T(8,128)(2,1)S(1)}) fusion(s32[1024]{0:T(1024)S(1)} %iota_add_fusion), kind=kLoop, calls=%fused_computation.72 | loop fusion | flops 8388608 | bytes 2101248 | tf_op jit(solution)/shard_map/convert.5
  (327 shorter events, 133.3 us)
Async XLA Ops:
  8.6 5.8 %collective-permute-start.1 = (bf16[24,4]{0,1:T(4,128)(2,1)S(1)}, bf16[24,4]{0,1:T(4,128)(2,1)S(1)}, u32[]{:S(2)}, u32[]{:S(2)}) collective-permute-start(bf16[24,4]{0,1:T(4,128)(2,1)S(1)} %get-tuple-element.444), channel_id=1, source_target_pairs={{0,15},{1,0},{2,1},{3,2},{4,3},{5,4},{6,5},{7,6},{8,7},{9,8},{10,9... | collective-permute-start | bytes 584 | tf_op jit(solution)/shard_map/while/body/eval_jaxpr/ppermute | solution.py:14
  8.7 6.5 %collective-permute-start = (bf16[24,4,1024]{2,0,1:T(8,128)(2,1)S(1)}, bf16[24,4,1024]{2,0,1:T(8,128)(2,1)S(1)}, u32[]{:S(2)}, u32[]{:S(2)}) collective-permute-start(bf16[24,4,1024]{2,0,1:T(8,128)(2,1)S(1)} %get-tuple-element.443), channel_id=1, source_target_pairs={{0,15},{1,0},{2,1},{3,2},{4,3},{5,4},{6,5},{7,6},{8,7},{9,8},{10,9... | collective-permute-start | bytes 589832 | tf_op jit(solution)/shard_map/while/body/eval_jaxpr/ppermute | solution.py:14
  21.8 7.7 %collective-permute-start.1 = (bf16[24,4]{0,1:T(4,128)(2,1)S(1)}, bf16[24,4]{0,1:T(4,128)(2,1)S(1)}, u32[]{:S(2)}, u32[]{:S(2)}) collective-permute-start(bf16[24,4]{0,1:T(4,128)(2,1)S(1)} %get-tuple-element.444), channel_id=1, source_target_pairs={{0,15},{1,0},{2,1},{3,2},{4,3},{5,4},{6,5},{7,6},{8,7},{9,8},{10,9... | collective-permute-start | bytes 584 | tf_op jit(solution)/shard_map/while/body/eval_jaxpr/ppermute | solution.py:14
  24.7 5.7 %collective-permute-start = (bf16[24,4,1024]{2,0,1:T(8,128)(2,1)S(1)}, bf16[24,4,1024]{2,0,1:T(8,128)(2,1)S(1)}, u32[]{:S(2)}, u32[]{:S(2)}) collective-permute-start(bf16[24,4,1024]{2,0,1:T(8,128)(2,1)S(1)} %get-tuple-element.443), channel_id=1, source_target_pairs={{0,15},{1,0},{2,1},{3,2},{4,3},{5,4},{6,5},{7,6},{8,7},{9,8},{10,9... | collective-permute-start | bytes 589832 | tf_op jit(solution)/shard_map/while/body/eval_jaxpr/ppermute | solution.py:14
  36.9 7.1 %collective-permute-start.1 = (bf16[24,4]{0,1:T(4,128)(2,1)S(1)}, bf16[24,4]{0,1:T(4,128)(2,1)S(1)}, u32[]{:S(2)}, u32[]{:S(2)}) collective-permute-start(bf16[24,4]{0,1:T(4,128)(2,1)S(1)} %get-tuple-element.444), channel_id=1, source_target_pairs={{0,15},{1,0},{2,1},{3,2},{4,3},{5,4},{6,5},{7,6},{8,7},{9,8},{10,9... | collective-permute-start | bytes 584 | tf_op jit(solution)/shard_map/while/body/eval_jaxpr/ppermute | solution.py:14
  39.2 5.7 %collective-permute-start = (bf16[24,4,1024]{2,0,1:T(8,128)(2,1)S(1)}, bf16[24,4,1024]{2,0,1:T(8,128)(2,1)S(1)}, u32[]{:S(2)}, u32[]{:S(2)}) collective-permute-start(bf16[24,4,1024]{2,0,1:T(8,128)(2,1)S(1)} %get-tuple-element.443), channel_id=1, source_target_pairs={{0,15},{1,0},{2,1},{3,2},{4,3},{5,4},{6,5},{7,6},{8,7},{9,8},{10,9... | collective-permute-start | bytes 589832 | tf_op jit(solution)/shard_map/while/body/eval_jaxpr/ppermute | solution.py:14
  51.4 7.1 %collective-permute-start.1 = (bf16[24,4]{0,1:T(4,128)(2,1)S(1)}, bf16[24,4]{0,1:T(4,128)(2,1)S(1)}, u32[]{:S(2)}, u32[]{:S(2)}) collective-permute-start(bf16[24,4]{0,1:T(4,128)(2,1)S(1)} %get-tuple-element.444), channel_id=1, source_target_pairs={{0,15},{1,0},{2,1},{3,2},{4,3},{5,4},{6,5},{7,6},{8,7},{9,8},{10,9... | collective-permute-start | bytes 584 | tf_op jit(solution)/shard_map/while/body/eval_jaxpr/ppermute | solution.py:14
  53.7 5.7 %collective-permute-start = (bf16[24,4,1024]{2,0,1:T(8,128)(2,1)S(1)}, bf16[24,4,1024]{2,0,1:T(8,128)(2,1)S(1)}, u32[]{:S(2)}, u32[]{:S(2)}) collective-permute-start(bf16[24,4,1024]{2,0,1:T(8,128)(2,1)S(1)} %get-tuple-element.443), channel_id=1, source_target_pairs={{0,15},{1,0},{2,1},{3,2},{4,3},{5,4},{6,5},{7,6},{8,7},{9,8},{10,9... | collective-permute-start | bytes 589832 | tf_op jit(solution)/shard_map/while/body/eval_jaxpr/ppermute | solution.py:14
  65.9 7.1 %collective-permute-start.1 = (bf16[24,4]{0,1:T(4,128)(2,1)S(1)}, bf16[24,4]{0,1:T(4,128)(2,1)S(1)}, u32[]{:S(2)}, u32[]{:S(2)}) collective-permute-start(bf16[24,4]{0,1:T(4,128)(2,1)S(1)} %get-tuple-element.444), channel_id=1, source_target_pairs={{0,15},{1,0},{2,1},{3,2},{4,3},{5,4},{6,5},{7,6},{8,7},{9,8},{10,9... | collective-permute-start | bytes 584 | tf_op jit(solution)/shard_map/while/body/eval_jaxpr/ppermute | solution.py:14
  68.1 5.7 %collective-permute-start = (bf16[24,4,1024]{2,0,1:T(8,128)(2,1)S(1)}, bf16[24,4,1024]{2,0,1:T(8,128)(2,1)S(1)}, u32[]{:S(2)}, u32[]{:S(2)}) collective-permute-start(bf16[24,4,1024]{2,0,1:T(8,128)(2,1)S(1)} %get-tuple-element.443), channel_id=1, source_target_pairs={{0,15},{1,0},{2,1},{3,2},{4,3},{5,4},{6,5},{7,6},{8,7},{9,8},{10,9... | collective-permute-start | bytes 589832 | tf_op jit(solution)/shard_map/while/body/eval_jaxpr/ppermute | solution.py:14
  80.4 7.1 %collective-permute-start.1 = (bf16[24,4]{0,1:T(4,128)(2,1)S(1)}, bf16[24,4]{0,1:T(4,128)(2,1)S(1)}, u32[]{:S(2)}, u32[]{:S(2)}) collective-permute-start(bf16[24,4]{0,1:T(4,128)(2,1)S(1)} %get-tuple-element.444), channel_id=1, source_target_pairs={{0,15},{1,0},{2,1},{3,2},{4,3},{5,4},{6,5},{7,6},{8,7},{9,8},{10,9... | collective-permute-start | bytes 584 | tf_op jit(solution)/shard_map/while/body/eval_jaxpr/ppermute | solution.py:14
  82.6 5.7 %collective-permute-start = (bf16[24,4,1024]{2,0,1:T(8,128)(2,1)S(1)}, bf16[24,4,1024]{2,0,1:T(8,128)(2,1)S(1)}, u32[]{:S(2)}, u32[]{:S(2)}) collective-permute-start(bf16[24,4,1024]{2,0,1:T(8,128)(2,1)S(1)} %get-tuple-element.443), channel_id=1, source_target_pairs={{0,15},{1,0},{2,1},{3,2},{4,3},{5,4},{6,5},{7,6},{8,7},{9,8},{10,9... | collective-permute-start | bytes 589832 | tf_op jit(solution)/shard_map/while/body/eval_jaxpr/ppermute | solution.py:14
  94.9 7.1 %collective-permute-start.1 = (bf16[24,4]{0,1:T(4,128)(2,1)S(1)}, bf16[24,4]{0,1:T(4,128)(2,1)S(1)}, u32[]{:S(2)}, u32[]{:S(2)}) collective-permute-start(bf16[24,4]{0,1:T(4,128)(2,1)S(1)} %get-tuple-element.444), channel_id=1, source_target_pairs={{0,15},{1,0},{2,1},{3,2},{4,3},{5,4},{6,5},{7,6},{8,7},{9,8},{10,9... | collective-permute-start | bytes 584 | tf_op jit(solution)/shard_map/while/body/eval_jaxpr/ppermute | solution.py:14
  97.1 5.7 %collective-permute-start = (bf16[24,4,1024]{2,0,1:T(8,128)(2,1)S(1)}, bf16[24,4,1024]{2,0,1:T(8,128)(2,1)S(1)}, u32[]{:S(2)}, u32[]{:S(2)}) collective-permute-start(bf16[24,4,1024]{2,0,1:T(8,128)(2,1)S(1)} %get-tuple-element.443), channel_id=1, source_target_pairs={{0,15},{1,0},{2,1},{3,2},{4,3},{5,4},{6,5},{7,6},{8,7},{9,8},{10,9... | collective-permute-start | bytes 589832 | tf_op jit(solution)/shard_map/while/body/eval_jaxpr/ppermute | solution.py:14
  109.4 7.1 %collective-permute-start.1 = (bf16[24,4]{0,1:T(4,128)(2,1)S(1)}, bf16[24,4]{0,1:T(4,128)(2,1)S(1)}, u32[]{:S(2)}, u32[]{:S(2)}) collective-permute-start(bf16[24,4]{0,1:T(4,128)(2,1)S(1)} %get-tuple-element.444), channel_id=1, source_target_pairs={{0,15},{1,0},{2,1},{3,2},{4,3},{5,4},{6,5},{7,6},{8,7},{9,8},{10,9... | collective-permute-start | bytes 584 | tf_op jit(solution)/shard_map/while/body/eval_jaxpr/ppermute | solution.py:14
  111.6 5.7 %collective-permute-start = (bf16[24,4,1024]{2,0,1:T(8,128)(2,1)S(1)}, bf16[24,4,1024]{2,0,1:T(8,128)(2,1)S(1)}, u32[]{:S(2)}, u32[]{:S(2)}) collective-permute-start(bf16[24,4,1024]{2,0,1:T(8,128)(2,1)S(1)} %get-tuple-element.443), channel_id=1, source_target_pairs={{0,15},{1,0},{2,1},{3,2},{4,3},{5,4},{6,5},{7,6},{8,7},{9,8},{10,9... | collective-permute-start | bytes 589832 | tf_op jit(solution)/shard_map/while/body/eval_jaxpr/ppermute | solution.py:14
  123.8 7.1 %collective-permute-start.1 = (bf16[24,4]{0,1:T(4,128)(2,1)S(1)}, bf16[24,4]{0,1:T(4,128)(2,1)S(1)}, u32[]{:S(2)}, u32[]{:S(2)}) collective-permute-start(bf16[24,4]{0,1:T(4,128)(2,1)S(1)} %get-tuple-element.444), channel_id=1, source_target_pairs={{0,15},{1,0},{2,1},{3,2},{4,3},{5,4},{6,5},{7,6},{8,7},{9,8},{10,9... | collective-permute-start | bytes 584 | tf_op jit(solution)/shard_map/while/body/eval_jaxpr/ppermute | solution.py:14
  138.3 7.1 %collective-permute-start.1 = (bf16[24,4]{0,1:T(4,128)(2,1)S(1)}, bf16[24,4]{0,1:T(4,128)(2,1)S(1)}, u32[]{:S(2)}, u32[]{:S(2)}) collective-permute-start(bf16[24,4]{0,1:T(4,128)(2,1)S(1)} %get-tuple-element.444), channel_id=1, source_target_pairs={{0,15},{1,0},{2,1},{3,2},{4,3},{5,4},{6,5},{7,6},{8,7},{9,8},{10,9... | collective-permute-start | bytes 584 | tf_op jit(solution)/shard_map/while/body/eval_jaxpr/ppermute | solution.py:14
  140.6 5.7 %collective-permute-start = (bf16[24,4,1024]{2,0,1:T(8,128)(2,1)S(1)}, bf16[24,4,1024]{2,0,1:T(8,128)(2,1)S(1)}, u32[]{:S(2)}, u32[]{:S(2)}) collective-permute-start(bf16[24,4,1024]{2,0,1:T(8,128)(2,1)S(1)} %get-tuple-element.443), channel_id=1, source_target_pairs={{0,15},{1,0},{2,1},{3,2},{4,3},{5,4},{6,5},{7,6},{8,7},{9,8},{10,9... | collective-permute-start | bytes 589832 | tf_op jit(solution)/shard_map/while/body/eval_jaxpr/ppermute | solution.py:14
  152.8 7.1 %collective-permute-start.1 = (bf16[24,4]{0,1:T(4,128)(2,1)S(1)}, bf16[24,4]{0,1:T(4,128)(2,1)S(1)}, u32[]{:S(2)}, u32[]{:S(2)}) collective-permute-start(bf16[24,4]{0,1:T(4,128)(2,1)S(1)} %get-tuple-element.444), channel_id=1, source_target_pairs={{0,15},{1,0},{2,1},{3,2},{4,3},{5,4},{6,5},{7,6},{8,7},{9,8},{10,9... | collective-permute-start | bytes 584 | tf_op jit(solution)/shard_map/while/body/eval_jaxpr/ppermute | solution.py:14
  167.3 7.1 %collective-permute-start.1 = (bf16[24,4]{0,1:T(4,128)(2,1)S(1)}, bf16[24,4]{0,1:T(4,128)(2,1)S(1)}, u32[]{:S(2)}, u32[]{:S(2)}) collective-permute-start(bf16[24,4]{0,1:T(4,128)(2,1)S(1)} %get-tuple-element.444), channel_id=1, source_target_pairs={{0,15},{1,0},{2,1},{3,2},{4,3},{5,4},{6,5},{7,6},{8,7},{9,8},{10,9... | collective-permute-start | bytes 584 | tf_op jit(solution)/shard_map/while/body/eval_jaxpr/ppermute | solution.py:14
  181.8 7.1 %collective-permute-start.1 = (bf16[24,4]{0,1:T(4,128)(2,1)S(1)}, bf16[24,4]{0,1:T(4,128)(2,1)S(1)}, u32[]{:S(2)}, u32[]{:S(2)}) collective-permute-start(bf16[24,4]{0,1:T(4,128)(2,1)S(1)} %get-tuple-element.444), channel_id=1, source_target_pairs={{0,15},{1,0},{2,1},{3,2},{4,3},{5,4},{6,5},{7,6},{8,7},{9,8},{10,9... | collective-permute-start | bytes 584 | tf_op jit(solution)/shard_map/while/body/eval_jaxpr/ppermute | solution.py:14
  196.3 7.1 %collective-permute-start.1 = (bf16[24,4]{0,1:T(4,128)(2,1)S(1)}, bf16[24,4]{0,1:T(4,128)(2,1)S(1)}, u32[]{:S(2)}, u32[]{:S(2)}) collective-permute-start(bf16[24,4]{0,1:T(4,128)(2,1)S(1)} %get-tuple-element.444), channel_id=1, source_target_pairs={{0,15},{1,0},{2,1},{3,2},{4,3},{5,4},{6,5},{7,6},{8,7},{9,8},{10,9... | collective-permute-start | bytes 584 | tf_op jit(solution)/shard_map/while/body/eval_jaxpr/ppermute | solution.py:14
  210.8 7.1 %collective-permute-start.1 = (bf16[24,4]{0,1:T(4,128)(2,1)S(1)}, bf16[24,4]{0,1:T(4,128)(2,1)S(1)}, u32[]{:S(2)}, u32[]{:S(2)}) collective-permute-start(bf16[24,4]{0,1:T(4,128)(2,1)S(1)} %get-tuple-element.444), channel_id=1, source_target_pairs={{0,15},{1,0},{2,1},{3,2},{4,3},{5,4},{6,5},{7,6},{8,7},{9,8},{10,9... | collective-permute-start | bytes 584 | tf_op jit(solution)/shard_map/while/body/eval_jaxpr/ppermute | solution.py:14
  (6 other events, 34.1 us)
where the time goes:
time: 239 us; the launch traced here: 237 us
  other arithmetic  117 us (49%)
  starting transfers between devices  102 us (43%)
  waiting for transfers between devices  10.7 us (4%)
  local copies, waits for them, and re-layouts  3.79 us (2%)
    ppermute x30, starting transfers between devices, from_behind(): return lax.ppermute(value, axis, pairs)  102 us
    reduce_sum x32, other arithmetic, pair_beams(): forward = jnp.concatenate([jnp.sum(stack_re, 1), jnp.sum(stack_im, 1)], -1)  102 us
    ppermute x30, waiting for transfers between devices, from_behind(): return lax.ppermute(value, axis, pairs)  10.7 us
    another operation x1, other arithmetic  8.54 us
  transfers between devices with their start and end apart: 30, of which 15 were waited for; matrix products, arithmetic and copies ran while one was open for 2% of the time, Pallas kernels for 0%

commit v1 on v0

v1 whole, which is shorter than its diff:
```python
import functools
import math

import jax
import jax.numpy as jnp
from jax import lax
from jax.experimental import pallas as pl
from jax.experimental.pallas import tpu as pltpu
from jax.sharding import PartitionSpec as P

LAG = 1024
LANES = 128
ROWS = 8


def lag_table():
    fine = 16
    taps = jnp.arange(LAG, dtype=jnp.int32) - LAG // 2

    def small(bins):
        phase = bins[:, None] * taps[None, :] % LAG
        angle = phase.astype(jnp.float32) * (2.0 * math.pi / LAG)
        return lax.optimization_barrier((jnp.cos(angle), jnp.sin(angle)))

    c0, s0 = small(jnp.arange(fine, dtype=jnp.int32))
    c1, s1 = small(jnp.arange(LAG // 2 // fine, dtype=jnp.int32) * fine)
    cos = c1[:, None] * c0[None] - s1[:, None] * s0[None]
    sin = s1[:, None] * c0[None] + c1[:, None] * s0[None]
    both = jnp.concatenate([cos.reshape(-1, LAG), sin.reshape(-1, LAG)], 0)
    return both.astype(jnp.bfloat16)


def chip_of(place, chips, snake):
    if not snake:
        return place
    return jnp.where(place < chips // 2, 2 * place, 2 * (chips - 1 - place) + 1)


def place_of(chip, chips, snake):
    if not snake:
        return chip
    return jnp.where(chip % 2 == 0, chip // 2, chips - 1 - chip // 2)


def unpack(block, half):
    re = block[:, :half].astype(jnp.float32)
    im = block[:, half : 2 * half].astype(jnp.float32)
    count = block[:, 2 * half :].astype(jnp.float32)
    return re, im, lax.rsqrt(re * re + im * im + 0.25), count


def pair_kernel(
    n, snake, own_ref, beam_ref, slots, mine, seen, parts, back, back_out,
    fwd_send, fwd_recv, sib_send, sib_recv, back_send, back_recv,
):
    segs, stations, width = own_ref.shape
    half = (width - LANES) // 2
    chips = n // 2
    far = chips // 2
    band = lax.axis_index("band")
    me = lax.axis_index("blk")
    core = me % 2
    place = place_of(me // 2, chips, snake)

    def device(where, which):
        return chip_of(where % chips, chips, snake) * 2 + which

    left = device(place + chips - 1, core)
    sibling = device(place, 1 - core)

    barrier = pltpu.get_barrier_semaphore()
    for step in range(1, n):
        pl.semaphore_signal(
            barrier, inc=1, device_id=(band, (me + step) % n),
            device_id_type=pl.DeviceIdType.MESH,
        )
    pl.semaphore_wait(barrier, n - 1)

    def send_left(hop, source):
        return pltpu.make_async_remote_copy(
            src_ref=source, dst_ref=slots.at[2 * hop], send_sem=fwd_send.at[hop],
            recv_sem=fwd_recv.at[hop], device_id=(band, left),
            device_id_type=pl.DeviceIdType.MESH,
        )

    def send_sibling(hop, source):
        return pltpu.make_async_remote_copy(
            src_ref=source, dst_ref=slots.at[2 * hop + 1], send_sem=sib_send.at[hop],
            recv_sem=sib_recv.at[hop], device_id=(band, sibling),
            device_id_type=pl.DeviceIdType.MESH,
        )

    def send_back(slot, other):
        return pltpu.make_async_remote_copy(
            src_ref=back_out.at[slot], dst_ref=beam_ref.at[(me + n - other) % n],
            send_sem=back_send.at[slot], recv_sem=back_recv.at[slot],
            device_id=(band, other), device_id_type=pl.DeviceIdType.MESH,
        )

    send_left(1, own_ref).start()
    send_sibling(0, own_ref).start()

    for seg in range(segs):
        re, im, inv, count = unpack(own_ref[seg], half)
        for i in range(stations):
            for at, value in ((0, re), (half, im), (2 * half, inv), (3 * half, count)):
                size = value.shape[1]
                mine[i, seg, :, at : at + size] = jnp.broadcast_to(value[i : i + 1], (ROWS, size))

    def unit(block_ref, with_back):
        for seg in range(segs):
            re, im, inv, count = unpack(block_ref[seg], half)
            seen[seg, :, :half] = re
            seen[seg, :, half : 2 * half] = im
            seen[seg, :, 2 * half : 3 * half] = inv
            seen[seg, :, 3 * half :] = count
        if with_back:
            back[...] = jnp.zeros_like(back)

        def station(i, carry):
            weights = []
            for r in range(0, stations, ROWS):
                w = [
                    jnp.minimum(mine[i, s, :, 3 * half :], seen[s, r : r + ROWS, 3 * half :])
                    for s in range(segs)
                ]
                total = jnp.maximum(functools.reduce(jnp.add, w), 1.0)
                share = 1.0 / total
                weights.append([v * share for v in w])
            for c in range(0, half, LANES):
                own = [
                    [mine[i, s, :, at + c : at + c + LANES] for at in (0, half, 2 * half)]
                    for s in range(segs)
                ]
                ahead_re = ahead_im = None
                for index, r in enumerate(range(0, stations, ROWS)):
                    cross_re = cross_im = coh_re = coh_im = None
                    for s in range(segs):
                        ar, ai, ag = own[s]
                        br, bi, bg = [
                            seen[s, r : r + ROWS, at + c : at + c + LANES]
                            for at in (0, half, 2 * half)
                        ]
                        w = weights[index][s]
                        x = w * (ar * br + ai * bi)
                        y = w * (ai * br - ar * bi)
                        g = ag * bg
                        if s == 0:
                            cross_re, cross_im, coh_re, coh_im = x, y, g * x, g * y
                        else:
                            cross_re = cross_re + x
                            cross_im = cross_im + y
                            coh_re = coh_re + g * x
                            coh_im = coh_im + g * y
                    factor = coh_re * coh_re + coh_im * coh_im
                    stack_re = cross_re * factor
                    stack_im = cross_im * factor
                    if with_back:
                        back[r : r + ROWS, c : c + LANES] += stack_re
                        back[r : r + ROWS, half + c : half + c + LANES] -= stack_im
                    ahead_re = stack_re if index == 0 else ahead_re + stack_re
                    ahead_im = stack_im if index == 0 else ahead_im + stack_im
                parts[i, :, c : c + LANES] = ahead_re
                parts[i, :, half + c : half + c + LANES] = ahead_im
            return carry

        lax.fori_loop(0, stations, station, 0)

    def finish(other):
        beam_ref[(other + n - me) % n] = jnp.sum(parts[...], 1).astype(jnp.bfloat16)

    def return_back(slot, other):
        back_out[slot] = back[...].astype(jnp.bfloat16)
        send_back(slot, other).start()

    unit(own_ref, False)
    finish(me)
    send_left(1, own_ref).wait_recv()
    if far > 1:
        send_left(2, slots.at[2]).start()
    send_sibling(1, slots.at[2]).start()
    send_sibling(0, own_ref).wait_recv()
    unit(slots.at[1], False)
    finish(sibling)

    def stage(hop, carry):
        other = device(place + hop, core)
        unit(slots.at[2 * hop], True)
        finish(other)
        return_back(2 * hop, other)
        send_left(hop + 1, own_ref).wait_recv()

        @pl.when(hop + 1 < far)
        def _():
            send_left(hop + 2, slots.at[2 * hop + 2]).start()

        send_sibling(hop + 1, slots.at[2 * hop + 2]).start()
        other = device(place + hop, 1 - core)
        send_sibling(hop, own_ref).wait_recv()
        unit(slots.at[2 * hop + 1], True)
        finish(other)
        return_back(2 * hop + 1, other)
        return carry

    lax.fori_loop(1, far, stage, 0)
    send_sibling(far, own_ref).wait_recv()
    low = place < far
    pick = jnp.where(low, 0, 1)
    other = device(place + far, jnp.where(low, core, 1 - core))
    unit(slots.at[2 * far + pick], True)
    finish(other)
    return_back(2 * far, other)

    def drain(hop, carry):
        send_left(hop, own_ref).wait_send()
        send_sibling(hop, own_ref).wait_send()
        return carry

    send_sibling(0, own_ref).wait_send()
    lax.fori_loop(1, far + 1, drain, 0)

    def drain_back(slot, carry):
        send_back(slot, sibling).wait()
        return carry

    lax.fori_loop(2, 2 * far + 1, drain_back, 0)


def pair_beams(packed, n, snake):
    segs, stations, width = packed.shape
    half = (width - LANES) // 2
    far = n // 4
    dma = pltpu.SemaphoreType.DMA
    pairs = (n // 2 + 1) * stations * stations * half
    return pl.pallas_call(
        functools.partial(pair_kernel, n, snake),
        out_shape=jax.ShapeDtypeStruct((n, stations, 2 * half), jnp.bfloat16),
        in_specs=[pl.BlockSpec(memory_space=pltpu.VMEM)],
        out_specs=pl.BlockSpec(memory_space=pltpu.VMEM),
        scratch_shapes=[
            pltpu.VMEM((2 * far + 2, segs, stations, width), jnp.bfloat16),
            pltpu.VMEM((stations, segs, ROWS, 3 * half + LANES), jnp.float32),
            pltpu.VMEM((segs, stations, 3 * half + LANES), jnp.float32),
            pltpu.VMEM((stations, ROWS, 2 * half), jnp.float32),
            pltpu.VMEM((stations, 2 * half), jnp.float32),
            pltpu.VMEM((2 * far + 1, stations, 2 * half), jnp.bfloat16),
            dma((far + 1,)), dma((far + 1,)), dma((far + 1,)), dma((far + 1,)),
            dma((2 * far + 1,)), dma((2 * far + 1,)),
        ],
        compiler_params=pltpu.CompilerParams(
            collective_id=0, has_side_effects=True, vmem_limit_bytes=48 * 1024 * 1024
        ),
        cost_estimate=pl.CostEstimate(
            flops=66 * pairs, bytes_accessed=2 * packed.size, transcendentals=0
        ),
        name="pair_beams",
    )(packed)


def shards(snake, spectra, counts):
    n = lax.axis_size("blk")
    stations, segs, spread = spectra.shape
    splat = jnp.broadcast_to(counts.astype(jnp.bfloat16)[:, :, None], (stations, segs, LANES))
    packed = jnp.concatenate([spectra, splat], 2).transpose(1, 0, 2)
    beams = pair_beams(packed, n, snake)
    table = lag_table()
    rows = jnp.dot(beams.reshape(-1, spread), table, preferred_element_type=jnp.float32)
    values = rows.astype(jnp.bfloat16).astype(jnp.float32)
    scale = jnp.sqrt(jnp.mean(values * values, -1, keepdims=True) + 1e-06)
    out = (values / scale).astype(jnp.bfloat16)
    return out.reshape(n, stations, LAG).transpose(1, 0, 2)


def solution(mesh):
    snake = mesh.shape["blk"] == 16
    return jax.shard_map(
        functools.partial(shards, snake),
        mesh=mesh,
        in_specs=(P(("band", "blk"), None, None), P(("band", "blk"), None)),
        out_specs=P(("band", "blk"), None, None),
        check_vma=False,
    )
```

time: 239 us -> 47.5 us (0.20)
  other arithmetic: 117 us -> 2.6 us
  starting transfers between devices: 102 us -> 0 us
  Pallas kernels: 0 us -> 41.2 us
  waiting for transfers between devices: 10.7 us -> 0 us
    ppermute x30 -> x0, starting transfers between devices: 102 us -> none  [from_behind(): return lax.ppermute(value, axis, pairs)]
    reduce_sum x32 -> x0, other arithmetic: 102 us -> none  [pair_beams(): forward = jnp.concatenate([jnp.sum(stack_re, 1), jnp.sum(stack_im, 1)], -1)]
    pallas_call x0 -> x1, Pallas kernels: none -> 41.2 us  [pair_beams(): pl.pallas_call(functools.partial(pair_kernel, n, snake), out_shape=jax.Sh...]
    ppermute x30 -> x0, waiting for transfers between devices: 10.7 us -> none  [from_behind(): return lax.ppermute(value, axis, pairs)]
    another operation x1, other arithmetic: 8.54 us -> 0.74 us
    mul x47 -> x1, other arithmetic: 3.38 us -> 0.01 us  [lag_table(): c1, s1 = small(jnp.arange(LAG // 2 // fine, dtype=jnp.int32) * fine)]
  transfers between devices with their start and end apart: 30 -> 0, of which waited for: 15 -> 0; matrix products, arithmetic and copies ran while one was open for 2% -> 0% of each run, Pallas kernels for 0% -> 0%
where the time goes in v1:
time: 47.5 us; the launch traced here: 47.3 us
  Pallas kernels  41.2 us (87%)
  other arithmetic  2.6 us (5%)
  local copies, waits for them, and re-layouts  2.38 us (5%)
  matrix products  1.09 us (2%)
    pallas_call x1, Pallas kernels, pair_beams(): pl.pallas_call(functools.partial(pair_kernel, n, snake), out_shape=jax.Sh...  41.2 us
    reshape x1, local copies, waits for them, and re-layouts, shards(): return out.reshape(n, stations, LAG).transpose(1, 0, 2)  1.32 us
    dot_general x1, matrix products, shards(): jnp.dot(beams.reshape(-1, spread), table, preferred_element_type=jnp.floa...  1.09 us
    unnamed x1, local copies, waits for them, and re-layouts  0.99 us

profile of v1, /device:TPU:1, one launch (start us, length us, event | category | flops | bytes accessed | tf_op | source)
XLA Modules:
  0.0 47.3 jit_solution(15762220408745132024)
XLA Ops:
  0.0 0.7 %convert_element_type.23 = bf16[24,4]{0,1:T(4,128)(2,1)S(1)} convert(s32[24,4]{0,1:T(4,128)} %param.3) | non-fusion elementwise | flops 96 | bytes 576 | tf_op jit(solution)/shard_map/convert_element_type | solution.py:263
  0.7 0.1 broadcast_in_dim.2
  0.8 0.3 fusion.20
  1.0 1.0 %copy.3 = bf16[24,4,1024]{2,0,1:T(8,128)(2,1)S(1)} copy(bf16[24,4,1024]{2,1,0:T(4,128)(2,1)} %param.2) | data formatting | bytes 393216 | tf_op args[0]
  2.1 0.6 %fusion.17 = (f32[32,1024]{1,0:T(8,128)S(1)}, f32[32,1024]{1,0:T(8,128)S(1)}) fusion(s32[1024]{0:T(1024)S(1)} %iota_add_fusion, s32[32]{0:T(128)S(1)} %iota_multiply_fusion), kind=kLoop, calls=%fused_computation.29 | loop fusion | flops 458752 | bytes 266368 | tf_op jit(solution)/shard_map/sin | solution.py:23
  2.7 41.2 %pair_beams.1 = bf16[16,24,1024]{2,1,0:T(8,128)(2,1)S(1)} custom-call(bf16[4,24,1152]{2,1,0:T(8,128)(2,1)S(1)} %maximum_bitcast_fusion.own_ref), custom_call_target="tpu_custom_call" | custom-call | flops 175177728 | bytes 221184 | tf_op jit(solution)/shard_map/pair_beams/pallas_call | solution.py:235
  43.9 0.7 %subtract_convert_fusion = (bf16[32,16,1024]{2,1,0:T(8,128)(2,1)S(1)}, bf16[32,16,1024]{2,1,0:T(8,128)(2,1)S(1)}) fusion(f32[16,1024]{1,0:T(8,128)S(1)} %get-tuple-element.12, f32[32,1024]{1,0:T(8,128)S(1)} %get-tuple-element.11, f32[16,1024]{1,0:T(8,128)S(1)} %get-tuple-element.10, f32[32,1024]{1,0:T(8,128)S(1)} %get-tuple-element.9), kind=kLoop, calls=%fused_computation.5 | loop fusion | flops 4194304 | bytes 2490368 | tf_op jit(solution)/shard_map/convert.3
  44.6 1.1 %fusion.4 = (f32[384]{0:T(512)S(1)}, bf16[384,1024]{1,0:T(8,128)(2,1)S(1)}) fusion(bf16[384,1024]{1,0:T(8,128)(2,1)S(1)} %bitcast.10, bf16[512,1024]{1,0:T(8,128)(2,1)S(1)} %bitcast.13, bf16[512,1024]{1,0:T(8,128)(2,1)S(1)} %bitcast.12), kind=kOutput, calls=%fused_computation.8 | convolution fusion | flops 811073152 | bytes 3671552 | tf_op jit(solution)/shard_map/dot_general | solution.py:267
  45.7 0.3 fusion.5
  46.0 1.3 %copy.6 = bf16[16,24,1024]{2,0,1:T(8,128)(2,1)} copy(bf16[16,24,1024]{2,1,0:T(8,128)(2,1)S(1)} %bitcast.11) | data formatting | bytes 1572864 | tf_op jit(solution)/shard_map/reshape | solution.py:271
  (4 shorter events, 0.0 us)

commit v2 on v1

v2 whole, which is shorter than its diff:
```python
import functools
import math

import jax
import jax.numpy as jnp
from jax import lax
from jax.experimental import pallas as pl
from jax.experimental.pallas import tpu as pltpu
from jax.sharding import PartitionSpec as P

LAG = 1024
WINS = 12
LANES = 128
ROWS = 8


def lag_table():
    fine = 16
    taps = jnp.arange(LAG, dtype=jnp.int32) - LAG // 2

    def small(bins):
        phase = bins[:, None] * taps[None, :] % LAG
        angle = phase.astype(jnp.float32) * (2.0 * math.pi / LAG)
        return lax.optimization_barrier((jnp.cos(angle), jnp.sin(angle)))

    c0, s0 = small(jnp.arange(fine, dtype=jnp.int32))
    c1, s1 = small(jnp.arange(LAG // 2 // fine, dtype=jnp.int32) * fine)
    cos = c1[:, None] * c0[None] - s1[:, None] * s0[None]
    sin = s1[:, None] * c0[None] + c1[:, None] * s0[None]
    cos, sin = cos.reshape(2, -1, LAG), sin.reshape(2, -1, LAG)
    both = jnp.concatenate([cos[0], sin[0], cos[1], sin[1]], 0)
    return both.astype(jnp.bfloat16)


def chip_of(place, chips, snake):
    if not snake:
        return place
    return jnp.where(place < chips // 2, 2 * place, 2 * (chips - 1 - place) + 1)


def place_of(chip, chips, snake):
    if not snake:
        return chip
    return jnp.where(chip % 2 == 0, chip // 2, chips - 1 - chip // 2)


def pair_kernel(
    n, snake, levels, own_ref, splat_ref, flat_ref, beam_ref, slots, table, weight, norm, seen,
    ahead, parts, back_out, counts_in, counts, fwd_send, fwd_recv, sib_send, sib_recv,
    back_send, back_recv, count_send, count_recv, local_sem,
):
    rows, width = own_ref.shape[1:]
    stations = beam_ref.shape[2]
    segs = rows // stations
    part = width // 2
    chips = n // 2
    far = chips // 2
    band = lax.axis_index("band")
    me = lax.axis_index("blk")
    core = me % 2
    place = place_of(me // 2, chips, snake)
    low = place < far
    mesh_id = pl.DeviceIdType.MESH

    def device(where, which):
        return chip_of(where % chips, chips, snake) * 2 + which

    left = device(place + chips - 1, core)
    right = device(place + 1, core)
    sibling = device(place, 1 - core)
    ways = ((0, left), (1, right))

    barrier = pltpu.get_barrier_semaphore()
    for step in range(1, n):
        pl.semaphore_signal(barrier, inc=1, device_id=(band, (me + step) % n), device_id_type=mesh_id)
    pl.semaphore_wait(barrier, n - 1)

    def hand_on(way, hop, source, target):
        return pltpu.make_async_remote_copy(
            src_ref=source, dst_ref=slots.at[way, 2 * hop], send_sem=fwd_send.at[way, hop],
            recv_sem=fwd_recv.at[way, hop], device_id=(band, target), device_id_type=mesh_id,
        )

    def share(way, hop, source):
        return pltpu.make_async_remote_copy(
            src_ref=source, dst_ref=slots.at[way, 2 * hop + 1], send_sem=sib_send.at[way, hop],
            recv_sem=sib_recv.at[way, hop], device_id=(band, sibling), device_id_type=mesh_id,
        )

    def give_back(way, slot, other):
        return pltpu.make_async_remote_copy(
            src_ref=back_out.at[way, slot], dst_ref=beam_ref.at[way, (me + n - other) % n],
            send_sem=back_send.at[way, slot], recv_sem=back_recv.at[way, slot],
            device_id=(band, other), device_id_type=mesh_id,
        )

    def tell(step):
        return pltpu.make_async_remote_copy(
            src_ref=flat_ref, dst_ref=counts_in.at[me], send_sem=count_send.at[step],
            recv_sem=count_recv.at[step], device_id=(band, (me + step) % n), device_id_type=mesh_id,
        )

    for step in range(1, n):
        tell(step).start()
    for way, target in ways:
        hand_on(way, 1, own_ref.at[way], target).start()
    share(1 - core, 0, own_ref.at[1 - core]).start()

    def unpack(block):
        re = block[:, :part].astype(jnp.float32)
        im = block[:, part:].astype(jnp.float32)
        return re, im, lax.rsqrt(re * re + im * im + 0.25)

    counts_in[me] = flat_ref[...]
    for way in range(2):
        re, im, inv = unpack(own_ref[way])
        norm[way] = inv
        for level in range(levels):
            held = jnp.minimum(splat_ref[...], float(level))
            if way == 0:
                weight[level] = held
            for c in range(0, part, LANES):
                table[way, level, :, c : c + LANES] = held * re[:, c : c + LANES]
                table[way, level, :, part + c : part + c + LANES] = held * im[:, c : c + LANES]
    for step in range(1, n):
        tell(step).wait()
    to_scalars = pltpu.make_async_copy(counts_in, counts, local_sem)
    to_scalars.start()
    to_scalars.wait()

    def unit(way, block_ref, other, slot):
        re, im, inv = unpack(block_ref[...])
        for c in range(0, part, LANES):
            seen[c // LANES] = re[:, c : c + LANES]
            seen[(part + c) // LANES] = im[:, c : c + LANES]
            seen[(2 * part + c) // LANES] = inv[:, c : c + LANES]
        ahead[...] = jnp.zeros_like(ahead)

        def station(j, carry):
            level = [counts[other, 0, j * segs + s] for s in range(segs)]
            shares = []
            for r in range(0, stations, ROWS):
                total = functools.reduce(
                    jnp.add,
                    [
                        weight[level[s], s * stations + r : s * stations + r + ROWS, :]
                        for s in range(segs)
                    ],
                )
                one = 1.0 / jnp.maximum(total, 1.0)
                shares.append(one * one * one)
            for c in range(0, part, LANES):
                theirs = [
                    [
                        seen[(at + c) // LANES, pl.ds(s * stations + j, ROWS, stride=0), :]
                        for at in (0, part, 2 * part)
                    ]
                    for s in range(segs)
                ]
                behind_re = behind_im = None
                for index, r in enumerate(range(0, stations, ROWS)):
                    cross_re = cross_im = coh_re = coh_im = None
                    for s in range(segs):
                        at = s * stations + r
                        ar = table[way, level[s], at : at + ROWS, c : c + LANES]
                        ai = table[way, level[s], at : at + ROWS, part + c : part + c + LANES]
                        ag = norm[way, at : at + ROWS, c : c + LANES]
                        br, bi, bg = theirs[s]
                        x = ar * br + ai * bi
                        y = ai * br - ar * bi
                        g = ag * bg
                        if s == 0:
                            cross_re, cross_im, coh_re, coh_im = x, y, g * x, g * y
                        else:
                            cross_re = cross_re + x
                            cross_im = cross_im + y
                            coh_re = coh_re + g * x
                            coh_im = coh_im + g * y
                    factor = (coh_re * coh_re + coh_im * coh_im) * shares[index]
                    stack_re = cross_re * factor
                    stack_im = cross_im * factor
                    ahead[r : r + ROWS, c : c + LANES] += stack_re
                    ahead[r : r + ROWS, part + c : part + c + LANES] += stack_im
                    behind_re = stack_re if index == 0 else behind_re + stack_re
                    behind_im = stack_im if index == 0 else behind_im + stack_im
                if slot is not None:
                    parts[j, :, c : c + LANES] = behind_re
                    parts[j, :, part + c : part + c + LANES] = -behind_im
            return carry

        lax.fori_loop(0, stations, station, 0)
        beam_ref[way, (other + n - me) % n] = ahead[...].astype(jnp.bfloat16)
        if slot is not None:
            back_out[way, slot] = jnp.sum(parts[...], 1).astype(jnp.bfloat16)
            give_back(way, slot, other).start()

    def own_unit(way, carry):
        unit(way, own_ref.at[way], me, None)
        return carry

    lax.fori_loop(0, 2, own_unit, 0)

    def pass_on(hop):
        for way, target in ways:
            here = slots.at[way, 2 * hop]
            hand_on(way, hop, here, target).wait_recv()
            wanted = (hop + 1 < far) | ((hop + 1 == far) & last_wanted[way])

            @pl.when(wanted)
            def _():
                hand_on(way, hop + 1, here, target).start()

            share(way, hop, here).start()

    last_wanted = (
        (place + chips - 1) % chips < far,
        (place + 1) % chips >= far,
    )
    last_way = jnp.where(low, 0, 1)

    pass_on(1)
    share(core, 0, own_ref.at[core]).wait_recv()
    unit(core, slots.at[core, 1], sibling, 1)

    def stage(hop, carry):
        def both(way, carry):
            where = place + jnp.where(way == 0, hop, chips - hop)
            unit(way, slots.at[way, 2 * hop], device(where, core), 2 * hop)
            return carry

        def both_shared(way, carry):
            where = place + jnp.where(way == 0, hop, chips - hop)
            share(way, hop, own_ref.at[way]).wait_recv()
            unit(way, slots.at[way, 2 * hop + 1], device(where, 1 - core), 2 * hop + 1)
            return carry

        lax.fori_loop(0, 2, both, 0)

        @pl.when(hop + 1 < far)
        def _():
            pass_on(hop + 1)

        @pl.when(hop + 1 == far)
        def _():
            here = slots.at[last_way, 2 * far]
            hand_on(last_way, far, here, left).wait_recv()
            share(last_way, far, here).start()

        lax.fori_loop(0, 2, both_shared, 0)
        return carry

    lax.fori_loop(1, far, stage, 0)
    unit(last_way, slots.at[last_way, 2 * far], device(place + far, core), 2 * far)
    share(last_way, far, own_ref.at[0]).wait_recv()
    unit(last_way, slots.at[last_way, 2 * far + 1], device(place + far, 1 - core), 2 * far + 1)

    share(1 - core, 0, own_ref.at[0]).wait_send()
    share(last_way, far, own_ref.at[0]).wait_send()
    give_back(core, 1, sibling).wait_send()
    give_back(1 - core, 1, sibling).wait_recv()
    for which in range(2):
        give_back(last_way, 2 * far + which, sibling).wait_send()
        give_back(1 - last_way, 2 * far + which, sibling).wait_recv()
    for way, target in ways:

        def drain(hop, carry):
            hand_on(way, hop, own_ref.at[0], target).wait_send()
            share(way, hop, own_ref.at[0]).wait_send()
            give_back(way, 2 * hop, sibling).wait()
            give_back(way, 2 * hop + 1, sibling).wait()
            return carry

        lax.fori_loop(1, far, drain, 0)

        @pl.when(last_wanted[way])
        def _():
            hand_on(way, far, own_ref.at[0], target).wait_send()


def pair_beams(packed, splat, flat, n, snake, levels):
    _, rows, width = packed.shape
    segs = 4
    stations = rows // segs
    part = width // 2
    far = n // 4
    dma = pltpu.SemaphoreType.DMA
    pairs = (n // 2 + 1) * stations * stations * 2 * part
    vmem = pl.BlockSpec(memory_space=pltpu.VMEM)
    return pl.pallas_call(
        functools.partial(pair_kernel, n, snake, levels),
        out_shape=jax.ShapeDtypeStruct((2, n, stations, width), jnp.bfloat16),
        in_specs=[vmem, vmem, vmem],
        out_specs=vmem,
        scratch_shapes=[
            pltpu.VMEM((2, 2 * far + 2, rows, width), jnp.bfloat16),
            pltpu.VMEM((2, levels, rows, width), jnp.float32),
            pltpu.VMEM((levels, rows, LANES), jnp.float32),
            pltpu.VMEM((2, rows, part), jnp.float32),
            pltpu.VMEM((3 * part // LANES, rows, LANES), jnp.float32),
            pltpu.VMEM((stations, width), jnp.float32),
            pltpu.VMEM((stations, ROWS, width), jnp.float32),
            pltpu.VMEM((2, 2 * far + 2, stations, width), jnp.bfloat16),
            pltpu.VMEM((n, 1, LANES), jnp.int32),
            pltpu.SMEM((n, 1, LANES), jnp.int32),
            dma((2, far + 1)), dma((2, far + 1)), dma((2, far + 1)), dma((2, far + 1)),
            dma((2, 2 * far + 2)), dma((2, 2 * far + 2)), dma((n,)), dma((n,)), dma,
        ],
        compiler_params=pltpu.CompilerParams(
            collective_id=0, has_side_effects=True, vmem_limit_bytes=56 * 1024 * 1024
        ),
        cost_estimate=pl.CostEstimate(
            flops=60 * pairs, bytes_accessed=2 * packed.size, transcendentals=0
        ),
        name="pair_beams",
    )(packed, splat, flat)


def shards(snake, spectra, counts):
    n = lax.axis_size("blk")
    stations, segs, spread = spectra.shape
    packed = spectra.reshape(stations, segs, 2, 2, spread // 4).transpose(3, 1, 0, 2, 4)
    packed = packed.reshape(2, segs * stations, spread // 2)
    splat = jnp.broadcast_to(
        counts.astype(jnp.float32).T.reshape(-1, 1), (segs * stations, LANES)
    )
    flat = jnp.pad(counts.reshape(1, -1), ((0, 0), (0, LANES - counts.size)))
    beams = pair_beams(packed, splat, flat, n, snake, WINS + 1)
    table = lag_table()
    halves = beams.reshape(2, n * stations, spread // 2)
    rows = jnp.dot(halves[0], table[: spread // 2], preferred_element_type=jnp.float32)
    rows += jnp.dot(halves[1], table[spread // 2 :], preferred_element_type=jnp.float32)
    values = rows.astype(jnp.bfloat16).astype(jnp.float32)
    scale = jnp.sqrt(jnp.mean(values * values, -1, keepdims=True) + 1e-06)
    out = (values / scale).astype(jnp.bfloat16)
    return out.reshape(n, stations, LAG).transpose(1, 0, 2)


def solution(mesh):
    snake = mesh.shape["blk"] == 16
    return jax.shard_map(
        functools.partial(shards, snake),
        mesh=mesh,
        in_specs=(P(("band", "blk"), None, None), P(("band", "blk"), None)),
        out_specs=P(("band", "blk"), None, None),
        check_vma=False,
    )
```

time: 47.5 us -> 56.4 us (1.19)
  Pallas kernels: 41.2 us -> 47 us
  local copies, waits for them, and re-layouts: 2.38 us -> 5.99 us
  other arithmetic: 2.6 us -> 1.9 us
    pallas_call x1, Pallas kernels: 41.2 us -> 47 us  [pair_beams(): pl.pallas_call(functools.partial(pair_kernel, n, snake, levels), out_shap...]
    slice x0 -> x2, local copies, waits for them, and re-layouts: none -> 1.35 us  [the longest x1 1.17 us: shards(): halves[1]]
    reshape x0 -> x4, local copies, waits for them, and re-layouts: none -> 1.13 us  [the longest x1 0.81 us: shards(): packed = packed.reshape(2, segs * stations, spread // 2)]
    broadcast_in_dim x1 -> x2, local copies, waits for them, and re-layouts: 0.07 us -> 0.79 us  [shards(): jnp.broadcast_to(counts.astype(jnp.float32).T.reshape(-1, 1), (segs * sta...]
    convert_element_type x1 -> x0, other arithmetic: 0.68 us -> none  [shards(): counts.astype(jnp.bfloat16)[:, :, None]]
    pad x0 -> x1, local copies, waits for them, and re-layouts: none -> 0.59 us  [shards(): flat = jnp.pad(counts.reshape(1, -1), ((0, 0), (0, LANES - counts.size)))]
    dot_general x1 -> x2, matrix products: 1.09 us -> 1.25 us  [the longest x1 0.68 us: shards(): jnp.dot(halves[1], table[spread // 2:], preferred_element_type=jnp.float32)]
where the time goes in v2:
time: 56.4 us; the launch traced here: 56.3 us
  Pallas kernels  47 us (83%)
  local copies, waits for them, and re-layouts  5.99 us (11%)
  other arithmetic  1.9 us (3%)
  matrix products  1.25 us (2%)
    pallas_call x1, Pallas kernels, pair_beams(): pl.pallas_call(functools.partial(pair_kernel, n, snake, levels), out_shap...  47 us
    reshape x1, local copies, waits for them, and re-layouts, shards(): return out.reshape(n, stations, LAG).transpose(1, 0, 2)  1.32 us
    slice x1, local copies, waits for them, and re-layouts, shards(): halves[1]  1.17 us

profile of v2, /device:TPU:1, one launch (start us, length us, event | category | flops | bytes accessed | tf_op | source)
XLA Modules:
  0.0 56.3 jit_solution(13720934787493715637)
XLA Ops:
  0.0 0.6 %fusion.17 = (f32[32,1024]{1,0:T(8,128)S(1)}, f32[32,1024]{1,0:T(8,128)S(1)}) fusion(s32[1024]{0:T(1024)S(1)} %iota_add_fusion, s32[32]{0:T(128)S(1)} %iota_multiply_fusion), kind=kLoop, calls=%fused_computation.32 | loop fusion | flops 458752 | bytes 266368 | tf_op jit(solution)/shard_map/sin | solution.py:24
  0.6 0.3 fusion.20
  0.9 0.7 %subtract_convert_fusion = (bf16[32,16,1024]{2,1,0:T(8,128)(2,1)S(1)}, bf16[32,16,1024]{2,1,0:T(8,128)(2,1)S(1)}) fusion(f32[16,1024]{1,0:T(8,128)S(1)} %get-tuple-element.12, f32[32,1024]{1,0:T(8,128)S(1)} %get-tuple-element.11, f32[16,1024]{1,0:T(8,128)S(1)} %get-tuple-element.10, f32[32,1024]{1,0:T(8,128)S(1)} %get-tuple-element.9), kind=kLoop, calls=%fused_computation.1 | loop fusion | flops 4194304 | bytes 2490368 | tf_op jit(solution)/shard_map/convert.11
  1.6 0.0 copy-start
  1.6 0.0 copy-start.1
  1.7 0.2 fusion.24
  1.8 0.7 %copy-done = bf16[24,4,1024]{2,1,0:T(4,128)(2,1)S(1)} copy-done((bf16[24,4,1024]{2,1,0:T(4,128)(2,1)S(1)}, bf16[24,4,1024]{2,1,0:T(4,128)(2,1)}, u32[]{:S(2)}) %copy-start) | copy-done | bytes 196632
  2.6 0.1 reshape.49
  2.6 0.2 copy.12
  2.8 0.8 %reshape.50.own_ref = bf16[2,96,512]{2,1,0:T(8,128)(2,1)} reshape(bf16[2,4,24,2,256]{4,3,2,1,0:T(2,128)(2,1)S(1)} %bitcast.21) | data formatting | bytes 393216 | tf_op jit(solution)/shard_map/reshape | solution.py:322
  3.6 0.0 copy-done.1
  3.6 0.1 broadcast_in_dim.4
  3.7 0.7 %broadcast_in_dim.5.splat_ref = f32[96,128]{1,0:T(8,128)} broadcast(f32[96]{0:T(128)S(1)} %broadcast_in_dim.4), dimensions={0} | broadcast | bytes 49536 | tf_op jit(solution)/shard_map/broadcast_in_dim | solution.py:323
  4.4 0.1 copy.7
  4.5 0.1 reshape.51
  4.6 0.6 %pad.4.flat_ref = s32[1,128]{1,0:T(1,128)} pad(s32[1,96]{1,0:T(1,128)S(1)} %reshape.51, s32[]{:T(128)} %constant.30.clone.1), padding=0_0x0_32 | pad | bytes 900 | tf_op jit(solution)/shard_map/jit(_pad)/pad | solution.py:326
  5.2 47.0 %pair_beams.1 = bf16[2,16,24,512]{3,2,1,0:T(8,128)(2,1)} custom-call(bf16[2,96,512]{2,1,0:T(8,128)(2,1)} %reshape.50.own_ref, f32[96,128]{1,0:T(8,128)} %broadcast_in_dim.5.splat_ref, s32[1,128]{1,0:T(1,128)} %pad.4.flat_ref), custom_call_target="tpu_custom_call" | custom-call | flops 159252480 | bytes 196608 | tf_op jit(solution)/shard_map/pair_beams/pallas_call | solution.py:289
  52.2 1.2 %fusion.26 = (bf16[1,16,24,512]{3,2,1,0:T(8,128)(2,1)S(1)}, bf16[1,16,24,512]{3,2,1,0:T(8,128)(2,1)S(1)}) fusion(bf16[2,16,24,512]{3,2,1,0:T(8,128)(2,1)} %pair_beams.1), kind=kLoop, calls=%fused_computation.45 | loop fusion | bytes 1572864 | tf_op jit(solution)/shard_map/slice | solution.py:331
  53.4 0.6 %fusion.2 = f32[384,1024]{1,0:T(8,128)S(1)} fusion(bf16[384,512]{1,0:T(8,128)(2,1)S(1)} %bitcast.20, bf16[256,1024]{1,0:T(8,128)(2,1)S(1)} %bitcast.19, bf16[256,1024]{1,0:T(8,128)(2,1)S(1)} %bitcast.18), kind=kOutput, calls=%fused_computation.7 | convolution fusion | flops 404750336 | bytes 3014656 | tf_op jit(solution)/shard_map/dot_general | solution.py:330
  54.0 0.7 %fusion = (f32[384]{0:T(512)S(1)}, bf16[384,1024]{1,0:T(8,128)(2,1)S(1)}) fusion(f32[384,1024]{1,0:T(8,128)S(1)} %fusion.2, bf16[384,512]{1,0:T(8,128)(2,1)S(1)} %bitcast.24, bf16[256,1024]{1,0:T(8,128)(2,1)S(1)} %bitcast.23, bf16[256,1024]{1,0:T(8,128)(2,1)S(1)} %bitcast.22), kind=kOutput, calls=%fused_computation.4 | convolution fusion | flops 406716032 | bytes 3802624 | tf_op jit(solution)/shard_map/dot_general | solution.py:331
  54.7 0.3 fusion.1
  54.9 1.3 %copy.11 = bf16[16,24,1024]{2,0,1:T(8,128)(2,1)} copy(bf16[16,24,1024]{2,1,0:T(8,128)(2,1)S(1)} %bitcast.17) | data formatting | bytes 1572864 | tf_op jit(solution)/shard_map/reshape | solution.py:335
  (4 shorter events, 0.0 us)
Async XLA Ops:
  1.6 0.9 %copy-start = (bf16[24,4,1024]{2,1,0:T(4,128)(2,1)S(1)}, bf16[24,4,1024]{2,1,0:T(4,128)(2,1)}, u32[]{:S(2)}) copy-start(bf16[24,4,1024]{2,1,0:T(4,128)(2,1)} %param.2) | copy-start | bytes 589828
  1.6 2.0 %copy-start.1 = (s32[24,4]{0,1:T(4,128)S(1)}, s32[24,4]{0,1:T(4,128)}, u32[]{:S(2)}) copy-start(s32[24,4]{0,1:T(4,128)} %param.3) | copy-start | bytes 1156

commit v3 on v1

--- a/solution.py
+++ b/solution.py
@@ -164,7 +164,7 @@
                 parts[i, :, half + c : half + c + LANES] = ahead_im
             return carry
 
-        lax.fori_loop(0, stations, station, 0)
+        lax.fori_loop(0, stations, station, 0, unroll=2)
 
     def finish(other):
         beam_ref[(other + n - me) % n] = jnp.sum(parts[...], 1).astype(jnp.bfloat16)
@@ -179,9 +179,6 @@
     if far > 1:
         send_left(2, slots.at[2]).start()
     send_sibling(1, slots.at[2]).start()
-    send_sibling(0, own_ref).wait_recv()
-    unit(slots.at[1], False)
-    finish(sibling)
 
     def stage(hop, carry):
         other = device(place + hop, core)
@@ -210,6 +207,10 @@
     unit(slots.at[2 * far + pick], True)
     finish(other)
     return_back(2 * far, other)
+
+    send_sibling(0, own_ref).wait_recv()
+    unit(slots.at[1], False)
+    finish(sibling)
 
     def drain(hop, carry):
         send_left(hop, own_ref).wait_send()

time: 47.5 us -> 46.9 us (0.987)
  Pallas kernels: 41.2 us -> 40.6 us
    pallas_call x1, Pallas kernels: 41.2 us -> 40.6 us  [pair_beams(): pl.pallas_call(functools.partial(pair_kernel, n, snake), out_shape=jax.Sh...]
where the time goes in v3:
time: 46.9 us; the launch traced here: 46.7 us
  Pallas kernels  40.6 us (87%)
  other arithmetic  2.6 us (6%)
  local copies, waits for them, and re-layouts  2.38 us (5%)
  matrix products  1.09 us (2%)
    pallas_call x1, Pallas kernels, pair_beams(): pl.pallas_call(functools.partial(pair_kernel, n, snake), out_shape=jax.Sh...  40.6 us
    reshape x1, local copies, waits for them, and re-layouts, shards(): return out.reshape(n, stations, LAG).transpose(1, 0, 2)  1.32 us
    dot_general x1, matrix products, shards(): jnp.dot(beams.reshape(-1, spread), table, preferred_element_type=jnp.floa...  1.09 us
    unnamed x1, local copies, waits for them, and re-layouts  0.99 us

profile of v3, /device:TPU:1, one launch (start us, length us, event | category | flops | bytes accessed | tf_op | source)
XLA Modules:
  0.0 46.7 jit_solution(17066155295935413101)
XLA Ops:
  0.0 0.7 %convert_element_type.23 = bf16[24,4]{0,1:T(4,128)(2,1)S(1)} convert(s32[24,4]{0,1:T(4,128)} %param.3) | non-fusion elementwise | flops 96 | bytes 576 | tf_op jit(solution)/shard_map/convert_element_type | solution.py:264
  0.7 0.1 broadcast_in_dim.2
  0.8 0.3 fusion.20
  1.0 1.0 %copy.3 = bf16[24,4,1024]{2,0,1:T(8,128)(2,1)S(1)} copy(bf16[24,4,1024]{2,1,0:T(4,128)(2,1)} %param.2) | data formatting | bytes 393216 | tf_op args[0]
  2.1 0.6 %fusion.17 = (f32[32,1024]{1,0:T(8,128)S(1)}, f32[32,1024]{1,0:T(8,128)S(1)}) fusion(s32[1024]{0:T(1024)S(1)} %iota_add_fusion, s32[32]{0:T(128)S(1)} %iota_multiply_fusion), kind=kLoop, calls=%fused_computation.29 | loop fusion | flops 458752 | bytes 266368 | tf_op jit(solution)/shard_map/sin | solution.py:23
  2.7 40.6 %pair_beams.1 = bf16[16,24,1024]{2,1,0:T(8,128)(2,1)S(1)} custom-call(bf16[4,24,1152]{2,1,0:T(8,128)(2,1)S(1)} %maximum_bitcast_fusion.own_ref), custom_call_target="tpu_custom_call" | custom-call | flops 175177728 | bytes 221184 | tf_op jit(solution)/shard_map/pair_beams/pallas_call | solution.py:236
  43.3 0.7 %subtract_convert_fusion = (bf16[32,16,1024]{2,1,0:T(8,128)(2,1)S(1)}, bf16[32,16,1024]{2,1,0:T(8,128)(2,1)S(1)}) fusion(f32[16,1024]{1,0:T(8,128)S(1)} %get-tuple-element.12, f32[32,1024]{1,0:T(8,128)S(1)} %get-tuple-element.11, f32[16,1024]{1,0:T(8,128)S(1)} %get-tuple-element.10, f32[32,1024]{1,0:T(8,128)S(1)} %get-tuple-element.9), kind=kLoop, calls=%fused_computation.5 | loop fusion | flops 4194304 | bytes 2490368 | tf_op jit(solution)/shard_map/convert.3
  44.0 1.1 %fusion.4 = (f32[384]{0:T(512)S(1)}, bf16[384,1024]{1,0:T(8,128)(2,1)S(1)}) fusion(bf16[384,1024]{1,0:T(8,128)(2,1)S(1)} %bitcast.10, bf16[512,1024]{1,0:T(8,128)(2,1)S(1)} %bitcast.13, bf16[512,1024]{1,0:T(8,128)(2,1)S(1)} %bitcast.12), kind=kOutput, calls=%fused_computation.8 | convolution fusion | flops 811073152 | bytes 3671552 | tf_op jit(solution)/shard_map/dot_general | solution.py:268
  45.1 0.3 fusion.5
  45.4 1.3 %copy.6 = bf16[16,24,1024]{2,0,1:T(8,128)(2,1)} copy(bf16[16,24,1024]{2,1,0:T(8,128)(2,1)S(1)} %bitcast.11) | data formatting | bytes 1572864 | tf_op jit(solution)/shard_map/reshape | solution.py:272
  (4 shorter events, 0.0 us)

commit v4 on v3

--- a/solution.py
+++ b/solution.py
@@ -9,6 +9,7 @@
 from jax.sharding import PartitionSpec as P
 
 LAG = 1024
+SEGS = 4
 LANES = 128
 ROWS = 8
 
@@ -42,10 +43,13 @@
     return jnp.where(chip % 2 == 0, chip // 2, chips - 1 - chip // 2)
 
 
-def unpack(block, half):
-    re = block[:, :half].astype(jnp.float32)
-    im = block[:, half : 2 * half].astype(jnp.float32)
-    count = block[:, 2 * half :].astype(jnp.float32)
+def unpack(block_ref, seg, segs, half):
+    base = seg * 2 * half
+    last = segs * 2 * half
+    re = block_ref[:, base : base + half].astype(jnp.float32)
+    im = block_ref[:, base + half : base + 2 * half].astype(jnp.float32)
+    count = block_ref[:, last : last + LANES].astype(jnp.float32)[:, seg : seg + 1]
+    count = jnp.broadcast_to(count, (re.shape[0], LANES))
     return re, im, lax.rsqrt(re * re + im * im + 0.25), count
 
 
@@ -53,8 +57,9 @@
     n, snake, own_ref, beam_ref, slots, mine, seen, parts, back, back_out,
     fwd_send, fwd_recv, sib_send, sib_recv, back_send, back_recv,
 ):
-    segs, stations, width = own_ref.shape
-    half = (width - LANES) // 2
+    stations, width = own_ref.shape
+    segs = SEGS
+    half = (width - LANES) // (2 * segs)
     chips = n // 2
     far = chips // 2
     band = lax.axis_index("band")
@@ -101,7 +106,7 @@
     send_sibling(0, own_ref).start()
 
     for seg in range(segs):
-        re, im, inv, count = unpack(own_ref[seg], half)
+        re, im, inv, count = unpack(own_ref, seg, segs, half)
         for i in range(stations):
             for at, value in ((0, re), (half, im), (2 * half, inv), (3 * half, count)):
                 size = value.shape[1]
@@ -109,7 +114,7 @@
 
     def unit(block_ref, with_back):
         for seg in range(segs):
-            re, im, inv, count = unpack(block_ref[seg], half)
+            re, im, inv, count = unpack(block_ref, seg, segs, half)
             seen[seg, :, :half] = re
             seen[seg, :, half : 2 * half] = im
             seen[seg, :, 2 * half : 3 * half] = inv
@@ -228,8 +233,9 @@
 
 
 def pair_beams(packed, n, snake):
-    segs, stations, width = packed.shape
-    half = (width - LANES) // 2
+    stations, width = packed.shape
+    segs = SEGS
+    half = (width - LANES) // (2 * segs)
     far = n // 4
     dma = pltpu.SemaphoreType.DMA
     pairs = (n // 2 + 1) * stations * stations * half
@@ -239,7 +245,7 @@
         in_specs=[pl.BlockSpec(memory_space=pltpu.VMEM)],
         out_specs=pl.BlockSpec(memory_space=pltpu.VMEM),
         scratch_shapes=[
-            pltpu.VMEM((2 * far + 2, segs, stations, width), jnp.bfloat16),
+            pltpu.VMEM((2 * far + 2, stations, width), jnp.bfloat16),
             pltpu.VMEM((stations, segs, ROWS, 3 * half + LANES), jnp.float32),
             pltpu.VMEM((segs, stations, 3 * half + LANES), jnp.float32),
             pltpu.VMEM((stations, ROWS, 2 * half), jnp.float32),
@@ -261,8 +267,8 @@
 def shards(snake, spectra, counts):
     n = lax.axis_size("blk")
     stations, segs, spread = spectra.shape
-    splat = jnp.broadcast_to(counts.astype(jnp.bfloat16)[:, :, None], (stations, segs, LANES))
-    packed = jnp.concatenate([spectra, splat], 2).transpose(1, 0, 2)
+    lanes = jnp.pad(counts.astype(jnp.bfloat16), ((0, 0), (0, LANES - segs)))
+    packed = jnp.concatenate([spectra.reshape(stations, -1), lanes], 1)
     beams = pair_beams(packed, n, snake)
     table = lag_table()
     rows = jnp.dot(beams.reshape(-1, spread), table, preferred_element_type=jnp.float32)

time: 46.9 us -> 47.2 us (level)
  no operation moved by 1% of the time
where the time goes in v4:
time: 47.2 us; the launch traced here: 47.1 us
  Pallas kernels  41 us (87%)
  other arithmetic  2.59 us (5%)
  local copies, waits for them, and re-layouts  2.4 us (5%)
  matrix products  1.09 us (2%)
    pallas_call x1, Pallas kernels, pair_beams(): pl.pallas_call(functools.partial(pair_kernel, n, snake), out_shape=jax.Sh...  41 us
    reshape x1, local copies, waits for them, and re-layouts, shards(): return out.reshape(n, stations, LAG).transpose(1, 0, 2)  1.32 us
    dot_general x1, matrix products, shards(): jnp.dot(beams.reshape(-1, spread), table, preferred_element_type=jnp.floa...  1.09 us
    unnamed x1, local copies, waits for them, and re-layouts  0.99 us

profile of v4, /device:TPU:1, one launch (start us, length us, event | category | flops | bytes accessed | tf_op | source)
XLA Modules:
  0.0 47.1 jit_solution(2115985879720771201)
XLA Ops:
  0.0 0.7 %convert_element_type.25 = bf16[24,4]{0,1:T(4,128)(2,1)S(1)} convert(s32[24,4]{0,1:T(4,128)} %param.3) | non-fusion elementwise | flops 96 | bytes 576 | tf_op jit(solution)/shard_map/convert_element_type | solution.py:270
  0.7 0.1 copy.5
  0.8 0.3 fusion.22
  1.1 1.0 %copy.7 = bf16[3,8,4,1024]{3,1,2,0:T(8,128)(2,1)S(1)} copy(bf16[3,8,4,1024]{3,2,1,0:T(4,128)(2,1)} %bitcast.15) | data formatting | bytes 393216
  2.1 0.6 %fusion.19 = (f32[32,1024]{1,0:T(8,128)S(1)}, f32[32,1024]{1,0:T(8,128)S(1)}) fusion(s32[1024]{0:T(1024)S(1)} %iota_add_fusion, s32[32]{0:T(128)S(1)} %iota_multiply_fusion), kind=kLoop, calls=%fused_computation.31 | loop fusion | flops 458752 | bytes 266368 | tf_op jit(solution)/shard_map/sin | solution.py:24
  2.7 41.0 %pair_beams.1 = bf16[16,24,1024]{2,1,0:T(8,128)(2,1)S(1)} custom-call(bf16[24,4224]{1,0:T(8,128)(2,1)S(1)} %fusion.10.own_ref), custom_call_target="tpu_custom_call" | custom-call | flops 175177728 | bytes 202752 | tf_op jit(solution)/shard_map/pair_beams/pallas_call | solution.py:242
  43.6 0.7 %subtract_convert_fusion = (bf16[32,16,1024]{2,1,0:T(8,128)(2,1)S(1)}, bf16[32,16,1024]{2,1,0:T(8,128)(2,1)S(1)}) fusion(f32[16,1024]{1,0:T(8,128)S(1)} %get-tuple-element.12, f32[32,1024]{1,0:T(8,128)S(1)} %get-tuple-element.11, f32[16,1024]{1,0:T(8,128)S(1)} %get-tuple-element.10, f32[32,1024]{1,0:T(8,128)S(1)} %get-tuple-element.9), kind=kLoop, calls=%fused_computation.5 | loop fusion | flops 4194304 | bytes 2490368 | tf_op jit(solution)/shard_map/convert.3
  44.4 1.1 %fusion.4 = (f32[384]{0:T(512)S(1)}, bf16[384,1024]{1,0:T(8,128)(2,1)S(1)}) fusion(bf16[384,1024]{1,0:T(8,128)(2,1)S(1)} %bitcast.10, bf16[512,1024]{1,0:T(8,128)(2,1)S(1)} %bitcast.13, bf16[512,1024]{1,0:T(8,128)(2,1)S(1)} %bitcast.12), kind=kOutput, calls=%fused_computation.8 | convolution fusion | flops 811073152 | bytes 3671552 | tf_op jit(solution)/shard_map/dot_general | solution.py:274
  45.5 0.3 fusion.5
  45.8 1.3 %copy.9 = bf16[16,24,1024]{2,0,1:T(8,128)(2,1)} copy(bf16[16,24,1024]{2,1,0:T(8,128)(2,1)S(1)} %bitcast.11) | data formatting | bytes 1572864 | tf_op jit(solution)/shard_map/reshape | solution.py:278
  (4 shorter events, 0.0 us)
